TPU v7x, 512 devices: a whole 4x4x16 slice. The times are simulated.
512 devices in a mesh: obj: 16 (over x, z_hi, core), tile: 32 (over y, z_lo).
Axes of the slice: x: 4, y: 4, z: 16 (z_hi: 2, z_lo: 8; z = z_hi * 8 + z_lo), core: 2. Of those that a mesh axis runs over, the one named last changes fastest.
Arguments:
- checkpoints: bfloat16 [6, 12, 48, 32, 128], P(None, None, 'obj', 'tile'), may hold values from 0.19921875 to 2
- courant: float32 [2, 48, 32, 128], P(None, None, 'tile'), may hold values from -0.6 to 0.6
- insolation: float32 [32, 128], P('tile'), may hold values from 0.3 to 3
- region_mask: int32 [16, 32, 128], P('obj', 'tile'), may hold values 0 or 1
- measure_step: int32 [16], P('obj'), may hold values from 1 to 6
- snr_weight: float32 [12, 48], replicated, may hold values from 0.3 to 3
- diffusion_number: float32 [12, 47], replicated, may hold values from 0.1 to 2
- coupling: float32 [12, 12], replicated, may hold values from -1.75 to 1.75
- recombination: float32 [12], replicated, may hold values from 0.05 to 0.25
Outputs:
- state_adjoint: float32 [16, 12, 48, 32, 128], P('obj', None, None, 'tile')
- driver_grad: float32 [16, 6, 12, 48], P('obj')
All inputs are finite; a program needn't handle non-finite values. No bound on the sum of `region_mask` on one device may be relied on, other than what follows from the above.
Results may differ from a plain program's by a relative error of at most 0.0003.
Values may be sent and summed in bfloat16 or wider, within the bound.
A program may use at most 64 MiB of HBM per device.

v0:
```python
import jax
import jax.numpy as jnp
from jax import lax
from jax.sharding import PartitionSpec as P

smoothing = 0.2


def padded_2(block, sides, width):
    for axis, dim in sides:
        count = lax.axis_size(axis)
        forward = [(i, i + 1) for i in range(count - 1)]
        forward.append((count - 1, 0))
        backward = [(target, source) for source, target in forward]
        low = lax.ppermute(
            lax.slice_in_dim(block, block.shape[dim] - width, None, axis=dim), axis, forward
        )
        high = lax.ppermute(lax.slice_in_dim(block, 0, width, axis=dim), axis, backward)
        block = jnp.concatenate([low, block, high], axis=dim)
    return block


def advect_back(adjoint, padded, flux, northward):
    lat_pad = jnp.pad(adjoint, ((0, 0), (0, 0), (0, 0), (1, 1)))
    north_flux = jnp.pad(northward[None] * adjoint, ((0, 0), (0, 0), (0, 0), (1, 1)))
    beside_all = padded[:, :, 2:] + padded[:, :, :-2] + lat_pad[..., 2:] + lat_pad[..., :-2]
    carried = flux[:, :, 2:] - flux[:, :, :-2] + north_flux[..., 2:] - north_flux[..., :-2]
    return (1.0 - 4.0 * smoothing) * adjoint + smoothing * beside_all + 0.5 * carried


def react_back(solved, state, coupling, recombination):
    mixing = jnp.einsum("fg,...flxy->...glxy", coupling, solved, precision=lax.Precision.HIGHEST)
    return (
        solved
        + mixing
        - 2.0 * recombination[:, None, None, None] * state.astype(jnp.float32) * solved
    )


def per_device(
    checkpoints,
    courant,
    insolation,
    region_mask,
    measure_step,
    snr_weight,
    diffusion_number,
    coupling,
    recombination,
):
    steps = checkpoints.shape[0]
    fields, levels = snr_weight.shape
    width, latitudes = insolation.shape
    columns = width * latitudes
    cells = columns * lax.axis_size("tile")
    impulse = region_mask[0].astype(jnp.float32)[None, None] * snr_weight[:, :, None, None]
    below = jnp.pad(diffusion_number, ((0, 0), (1, 0)))
    above = jnp.pad(diffusion_number, ((0, 0), (0, 1)))
    middle = 1.0 + below + above
    eastward = courant[0]
    northward = courant[1]
    adjoint = jnp.zeros((fields, levels, width, latitudes), jnp.float32)
    partials = [None] * steps
    for back in range(steps):
        moment = steps - 1 - back
        arrive = (measure_step[0] == moment + 1).astype(jnp.float32)
        adjoint = adjoint + arrive * impulse
        stacked = jnp.stack([adjoint, eastward[None] * adjoint])
        extended = padded_2(stacked, (("tile", 3),), 1)
        padded = extended[0]
        flux = extended[1]
        advected = advect_back(adjoint, padded, flux, northward)
        solved = lax.linalg.tridiagonal_solve(
            -below, middle, -above, advected.reshape(fields, levels, columns)
        )
        solved = solved.reshape(fields, levels, width, latitudes)
        partial_sum = jnp.einsum("flxy,xy->fl", solved, insolation, precision=lax.Precision.HIGHEST)
        partial_sum = lax.psum(partial_sum, "tile")
        partials[moment] = partial_sum
        state = checkpoints[moment]
        adjoint = react_back(
            solved, lax.all_gather(state, "obj", axis=1, tiled=True), coupling, recombination
        )
    gradients = jnp.stack(partials)
    return (adjoint[None], (gradients / cells)[None])


def solution(mesh):
    return jax.shard_map(
        per_device,
        mesh=mesh,
        in_specs=(
            P(None, None, "obj", "tile", None),
            P(None, None, "tile", None),
            P("tile", None),
            P("obj", "tile", None),
            P("obj"),
            P(),
            P(),
            P(),
            P(),
        ),
        out_specs=(P("obj", None, None, "tile", None), P("obj", None, None, None)),
        check_vma=False,
    )
```

profile of v0, /device:TPU:6, one launch (start us, length us, event | category | flops | bytes accessed | tf_op | source)
XLA Modules:
  0.0 678.9 jit_solution(14576754906486607328)
XLA Ops:
  1.4 0.7 convert_bitcast_fusion
  2.0 0.8 copy.28
  2.8 0.8 fusion.1314
  4.0 15.6 %collective-permute-start.1 = (f32[2,12,48,1,128]{4,2,3,1,0:T(8,128)S(1)}, f32[2,12,48,1,128]{4,2,3,1,0:T(8,128)S(1)}, u32[]{:S(2)}, u32[]{:S(2)}) collective-permute-start(f32[2,12,48,1,128]{4,2,3,1,0:T(8,128)S(1)} %copy.30), channel_id=1, source_target_pairs={{1,0},{2,1},{3,2},{4,3},{5,4},{6,5},{7,6},{8,7},{9,8},{10,9},{11,1... | collective-permute-start | bytes 1769480 | tf_op jit(solution)/shard_map/ppermute | solution.py:18
  19.6 1.9 collective-permute-start
  22.8 53.8 %all-gather = bf16[1,12,48,1,128]{4,1,3,0,2:T(8,128)(2,1)S(1)} all-gather(bf16[1,12,3,1,128]{4,1,3,0,2:T(8,128)(2,1)S(1)} %copy.99), channel_id=2, replica_groups=mesh['obj'=16,'tile'=32] {'obj'}, dimensions={2}, use_global_device_ids=true | all-gather | bytes 156672 | tf_op jit(solution)/shard_map/all_gather | solution.py:82
  77.7 0.5 fusion.29
  78.2 0.5 fusion.1138
  81.4 0.6 fusion.13
  82.3 2.7 collective-permute-start.3
  85.0 3.1 collective-permute-start.2
  88.2 56.1 %all-gather.1 = bf16[1,12,48,1,128]{4,1,3,0,2:T(8,128)(2,1)S(1)} all-gather(bf16[1,12,3,1,128]{4,1,3,0,2:T(8,128)(2,1)S(1)} %copy.100), channel_id=3, replica_groups=mesh['obj'=16,'tile'=32] {'obj'}, dimensions={2}, use_global_device_ids=true | all-gather | bytes 156672 | tf_op jit(solution)/shard_map/all_gather | solution.py:82
  145.3 0.5 fusion.38
  145.8 0.5 fusion.959
  148.9 0.6 fusion.15
  149.9 4.9 collective-permute-start.5
  154.8 1.9 collective-permute-start.4
  156.8 57.8 %all-gather.2 = bf16[1,12,48,1,128]{4,1,3,0,2:T(8,128)(2,1)S(1)} all-gather(bf16[1,12,3,1,128]{4,1,3,0,2:T(8,128)(2,1)S(1)} %copy.101), channel_id=4, replica_groups=mesh['obj'=16,'tile'=32] {'obj'}, dimensions={2}, use_global_device_ids=true | all-gather | bytes 156672 | tf_op jit(solution)/shard_map/all_gather | solution.py:82
  216.0 0.5 fusion.786
  219.2 0.6 fusion.17
  220.1 5.1 collective-permute-start.7
  225.2 1.9 collective-permute-start.6
  227.2 58.4 %all-gather.5 = bf16[1,12,48,1,128]{4,1,3,0,2:T(8,128)(2,1)S(1)} all-gather(bf16[1,12,3,1,128]{4,1,3,0,2:T(8,128)(2,1)S(1)} %copy.104), channel_id=7, replica_groups=mesh['obj'=16,'tile'=32] {'obj'}, dimensions={2}, use_global_device_ids=true | all-gather | bytes 156672 | tf_op jit(solution)/shard_map/all_gather | solution.py:82
  285.6 34.4 %all-gather.3 = bf16[1,12,48,1,128]{4,1,3,0,2:T(8,128)(2,1)S(1)} all-gather(bf16[1,12,3,1,128]{4,1,3,0,2:T(8,128)(2,1)S(1)} %copy.102), channel_id=5, replica_groups=mesh['obj'=16,'tile'=32] {'obj'}, dimensions={2}, use_global_device_ids=true | all-gather | bytes 156672 | tf_op jit(solution)/shard_map/all_gather | solution.py:82
  320.0 44.8 %all-gather.4 = bf16[1,12,48,1,128]{4,1,3,0,2:T(8,128)(2,1)S(1)} all-gather(bf16[1,12,3,1,128]{4,1,3,0,2:T(8,128)(2,1)S(1)} %copy.103), channel_id=6, replica_groups=mesh['obj'=16,'tile'=32] {'obj'}, dimensions={2}, use_global_device_ids=true | all-gather | bytes 156672 | tf_op jit(solution)/shard_map/all_gather | solution.py:82
  364.9 0.9 fusion.84
  367.4 0.5 fusion.613
  370.5 0.6 fusion.19
  371.4 8.4 %collective-permute-start.9 = (f32[2,12,48,1,128]{4,2,3,1,0:T(8,128)S(1)}, f32[2,12,48,1,128]{4,2,3,1,0:T(8,128)S(1)}, u32[]{:S(2)}, u32[]{:S(2)}) collective-permute-start(f32[2,12,48,1,128]{4,2,3,1,0:T(8,128)S(1)} %copy.60), channel_id=1, source_target_pairs={{1,0},{2,1},{3,2},{4,3},{5,4},{6,5},{7,6},{8,7},{9,8},{10,9},{11,1... | collective-permute-start | bytes 1769480 | tf_op jit(solution)/shard_map/ppermute | solution.py:18
  379.9 2.1 collective-permute-start.8
  382.0 0.9 fusion.86
  383.1 0.9 fusion.88
  384.0 9.5 %collective-permute-done.9 = f32[2,12,48,1,128]{4,2,3,1,0:T(8,128)S(1)} collective-permute-done((f32[2,12,48,1,128]{4,2,3,1,0:T(8,128)S(1)}, f32[2,12,48,1,128]{4,2,3,1,0:T(8,128)S(1)}, u32[]{:S(2)}, u32[]{:S(2)}) %collective-permute-start.9) | collective-permute-done | bytes 589856 | tf_op jit(solution)/shard_map/ppermute | solution.py:18
  393.7 12.6 %collective-permute-done.8 = f32[2,12,48,1,128]{4,2,3,1,0:T(8,128)S(1)} collective-permute-done((f32[2,12,48,1,128]{4,2,3,1,0:T(8,128)S(1)}, f32[2,12,48,1,128]{4,2,3,1,0:T(8,128)S(1)}, u32[]{:S(2)}, u32[]{:S(2)}) %collective-permute-start.8) | collective-permute-done | bytes 589856 | tf_op jit(solution)/shard_map/ppermute | solution.py:15
  407.6 0.5 fusion.440
  410.7 0.6 fusion.21
  411.7 5.6 collective-permute-start.11
  417.2 1.9 collective-permute-start.10
  419.2 0.9 fusion.90
  420.2 0.9 fusion.92
  421.2 19.9 %collective-permute-done.11 = f32[2,12,48,1,128]{4,2,3,1,0:T(8,128)S(1)} collective-permute-done((f32[2,12,48,1,128]{4,2,3,1,0:T(8,128)S(1)}, f32[2,12,48,1,128]{4,2,3,1,0:T(8,128)S(1)}, u32[]{:S(2)}, u32[]{:S(2)}) %collective-permute-start.11) | collective-permute-done | bytes 589856 | tf_op jit(solution)/shard_map/ppermute | solution.py:18
  441.3 1.6 collective-permute-done.10
  444.2 0.5 fusion.267
  447.4 0.5 fusion.23
  447.9 1.0 copy.74
  448.9 0.9 fusion.94
  449.9 228.3 %all-reduce.14 = (f32[1,1,12,48]{3,0,2,1:T(1,128)S(1)}, f32[1,1,12,48]{3,0,2,1:T(1,128)S(1)}, f32[1,1,12,48]{3,0,2,1:T(1,128)S(1)}, f32[1,1,12,48]{3,0,2,1:T(1,1...) all-reduce(f32[1,1,12,48]{3,0,2,1:T(1,128)S(1)} %stack.87, ...), channel_id=1, replica_groups=mesh['obj'=16,'tile'=32] {'tile'}, use_global_device_ids=true, to_apply=%region_0.1 | all-reduce | flops 3456 | bytes 27648 | tf_op jit(solution)/shard_map/psum | solution.py:78
  678.3 0.7 broadcast_multiply_fusion.7
  (398 shorter events, 26.8 us)
Async XLA Ops:
  0.6 80.8 %copy-start = (f32[12,12]{1,0:T(8,128)S(1)}, f32[12,12]{1,0:T(8,128)}, u32[]{:S(2)}) copy-start(f32[12,12]{1,0:T(8,128)} %param.16) | copy-start | bytes 1732
  0.6 20.9 %copy-start.3 = (f32[12,47]{1,0:T(8,128)S(1)}, f32[12,47]{1,0:T(8,128)}, u32[]{:S(2)}) copy-start(f32[12,47]{1,0:T(8,128)} %param.15) | copy-start | bytes 6772
  0.7 21.1 %copy-start.1 = (bf16[6,12,3,1,128]{4,2,3,1,0:T(4,128)(2,1)S(1)}, bf16[6,12,3,1,128]{4,2,3,1,0:T(4,128)(2,1)}, u32[]{:S(2)}) copy-start(bf16[6,12,3,1,128]{4,2,3,1,0:T(4,128)(2,1)} %param.9) | copy-start | bytes 165892
  0.7 22.1 %copy-start.4 = (f32[12]{0:T(128)S(1)}, f32[12]{0:T(128)}, u32[]{:S(2)}) copy-start(f32[12]{0:T(128)} %param.17) | copy-start | bytes 148
  4.0 72.8 %collective-permute-start.1 = (f32[2,12,48,1,128]{4,2,3,1,0:T(8,128)S(1)}, f32[2,12,48,1,128]{4,2,3,1,0:T(8,128)S(1)}, u32[]{:S(2)}, u32[]{:S(2)}) collective-permute-start(f32[2,12,48,1,128]{4,2,3,1,0:T(8,128)S(1)} %copy.30), channel_id=1, source_target_pairs={{1,0},{2,1},{3,2},{4,3},{5,4},{6,5},{7,6},{8,7},{9,8},{10,9},{11,1... | collective-permute-start | bytes 1769480 | tf_op jit(solution)/shard_map/ppermute | solution.py:18
  19.6 57.4 %collective-permute-start = (f32[2,12,48,1,128]{4,2,3,1,0:T(8,128)S(1)}, f32[2,12,48,1,128]{4,2,3,1,0:T(8,128)S(1)}, u32[]{:S(2)}, u32[]{:S(2)}) collective-permute-start(f32[2,12,48,1,128]{4,2,3,1,0:T(8,128)S(1)} %copy.30), channel_id=1, source_target_pairs={{0,1},{1,2},{2,3},{3,4},{4,5},{5,6},{6,7},{7,8},{8,9},{9,10},{10,1... | collective-permute-start | bytes 1769480 | tf_op jit(solution)/shard_map/ppermute | solution.py:15
  82.3 62.0 %collective-permute-start.3 = (f32[2,12,48,1,128]{4,2,3,1,0:T(8,128)S(1)}, f32[2,12,48,1,128]{4,2,3,1,0:T(8,128)S(1)}, u32[]{:S(2)}, u32[]{:S(2)}) collective-permute-start(f32[2,12,48,1,128]{4,2,3,1,0:T(8,128)S(1)} %copy.39), channel_id=1, source_target_pairs={{1,0},{2,1},{3,2},{4,3},{5,4},{6,5},{7,6},{8,7},{9,8},{10,9},{11,1... | collective-permute-start | bytes 1769480 | tf_op jit(solution)/shard_map/ppermute | solution.py:18
  85.0 59.5 %collective-permute-start.2 = (f32[2,12,48,1,128]{4,2,3,1,0:T(8,128)S(1)}, f32[2,12,48,1,128]{4,2,3,1,0:T(8,128)S(1)}, u32[]{:S(2)}, u32[]{:S(2)}) collective-permute-start(f32[2,12,48,1,128]{4,2,3,1,0:T(8,128)S(1)} %copy.39), channel_id=1, source_target_pairs={{0,1},{1,2},{2,3},{3,4},{4,5},{5,6},{6,7},{7,8},{8,9},{9,10},{10,1... | collective-permute-start | bytes 1769480 | tf_op jit(solution)/shard_map/ppermute | solution.py:15
  149.9 64.7 %collective-permute-start.5 = (f32[2,12,48,1,128]{4,2,3,1,0:T(8,128)S(1)}, f32[2,12,48,1,128]{4,2,3,1,0:T(8,128)S(1)}, u32[]{:S(2)}, u32[]{:S(2)}) collective-permute-start(f32[2,12,48,1,128]{4,2,3,1,0:T(8,128)S(1)} %copy.46), channel_id=1, source_target_pairs={{1,0},{2,1},{3,2},{4,3},{5,4},{6,5},{7,6},{8,7},{9,8},{10,9},{11,1... | collective-permute-start | bytes 1769480 | tf_op jit(solution)/shard_map/ppermute | solution.py:18
  154.8 59.9 %collective-permute-start.4 = (f32[2,12,48,1,128]{4,2,3,1,0:T(8,128)S(1)}, f32[2,12,48,1,128]{4,2,3,1,0:T(8,128)S(1)}, u32[]{:S(2)}, u32[]{:S(2)}) collective-permute-start(f32[2,12,48,1,128]{4,2,3,1,0:T(8,128)S(1)} %copy.46), channel_id=1, source_target_pairs={{0,1},{1,2},{2,3},{3,4},{4,5},{5,6},{6,7},{7,8},{8,9},{9,10},{10,1... | collective-permute-start | bytes 1769480 | tf_op jit(solution)/shard_map/ppermute | solution.py:15
  219.8 145.1 %copy-start.2 = (f32[1,128]{1,0:T(1,128)S(1)}, f32[1,128]{1,0:T(1,128)}, u32[]{:S(2)}) copy-start(f32[1,128]{1,0:T(1,128)} %param.11) | copy-start | bytes 1540
  220.1 145.8 %collective-permute-start.7 = (f32[2,12,48,1,128]{4,2,3,1,0:T(8,128)S(1)}, f32[2,12,48,1,128]{4,2,3,1,0:T(8,128)S(1)}, u32[]{:S(2)}, u32[]{:S(2)}) collective-permute-start(f32[2,12,48,1,128]{4,2,3,1,0:T(8,128)S(1)} %copy.53), channel_id=1, source_target_pairs={{1,0},{2,1},{3,2},{4,3},{5,4},{6,5},{7,6},{8,7},{9,8},{10,9},{11,1... | collective-permute-start | bytes 1769480 | tf_op jit(solution)/shard_map/ppermute | solution.py:18
  225.2 140.9 %collective-permute-start.6 = (f32[2,12,48,1,128]{4,2,3,1,0:T(8,128)S(1)}, f32[2,12,48,1,128]{4,2,3,1,0:T(8,128)S(1)}, u32[]{:S(2)}, u32[]{:S(2)}) collective-permute-start(f32[2,12,48,1,128]{4,2,3,1,0:T(8,128)S(1)} %copy.53), channel_id=1, source_target_pairs={{0,1},{1,2},{2,3},{3,4},{4,5},{5,6},{6,7},{7,8},{8,9},{9,10},{10,1... | collective-permute-start | bytes 1769480 | tf_op jit(solution)/shard_map/ppermute | solution.py:15
  371.4 22.1 %collective-permute-start.9 = (f32[2,12,48,1,128]{4,2,3,1,0:T(8,128)S(1)}, f32[2,12,48,1,128]{4,2,3,1,0:T(8,128)S(1)}, u32[]{:S(2)}, u32[]{:S(2)}) collective-permute-start(f32[2,12,48,1,128]{4,2,3,1,0:T(8,128)S(1)} %copy.60), channel_id=1, source_target_pairs={{1,0},{2,1},{3,2},{4,3},{5,4},{6,5},{7,6},{8,7},{9,8},{10,9},{11,1... | collective-permute-start | bytes 1769480 | tf_op jit(solution)/shard_map/ppermute | solution.py:18
  379.9 26.5 %collective-permute-start.8 = (f32[2,12,48,1,128]{4,2,3,1,0:T(8,128)S(1)}, f32[2,12,48,1,128]{4,2,3,1,0:T(8,128)S(1)}, u32[]{:S(2)}, u32[]{:S(2)}) collective-permute-start(f32[2,12,48,1,128]{4,2,3,1,0:T(8,128)S(1)} %copy.60), channel_id=1, source_target_pairs={{0,1},{1,2},{2,3},{3,4},{4,5},{5,6},{6,7},{7,8},{8,9},{9,10},{10,1... | collective-permute-start | bytes 1769480 | tf_op jit(solution)/shard_map/ppermute | solution.py:15
  411.7 29.5 %collective-permute-start.11 = (f32[2,12,48,1,128]{4,2,3,1,0:T(8,128)S(1)}, f32[2,12,48,1,128]{4,2,3,1,0:T(8,128)S(1)}, u32[]{:S(2)}, u32[]{:S(2)}) collective-permute-start(f32[2,12,48,1,128]{4,2,3,1,0:T(8,128)S(1)} %copy.67), channel_id=1, source_target_pairs={{1,0},{2,1},{3,2},{4,3},{5,4},{6,5},{7,6},{8,7},{9,8},{10,9},{11,1... | collective-permute-start | bytes 1769480 | tf_op jit(solution)/shard_map/ppermute | solution.py:18
  417.2 25.7 %collective-permute-start.10 = (f32[2,12,48,1,128]{4,2,3,1,0:T(8,128)S(1)}, f32[2,12,48,1,128]{4,2,3,1,0:T(8,128)S(1)}, u32[]{:S(2)}, u32[]{:S(2)}) collective-permute-start(f32[2,12,48,1,128]{4,2,3,1,0:T(8,128)S(1)} %copy.67), channel_id=1, source_target_pairs={{0,1},{1,2},{2,3},{3,4},{4,5},{5,6},{6,7},{7,8},{8,9},{9,10},{10,1... | collective-permute-start | bytes 1769480 | tf_op jit(solution)/shard_map/ppermute | solution.py:15
where the time goes:
time: 680 us; the launch traced here: 679 us
  blocking collectives  534 us (79%)
  starting transfers between devices  55.3 us (8%)
  waiting for transfers between devices  43.6 us (6%)
  other arithmetic  26.3 us (4%)
  matrix products  9.1 us (1%)
  local copies, waits for them, and re-layouts  8.41 us (1%)
    all_gather x6, blocking collectives, per_device(): lax.all_gather(state, 'obj', axis=1, tiled=True)  305 us
    psum x1, blocking collectives, per_device(): partial_sum = lax.psum(partial_sum, 'tile')  228 us
    ppermute x6, starting transfers between devices, padded_2(): lax.ppermute(lax.slice_in_dim(block, 0, width, axis=dim), axis, backward)  42.3 us
    ppermute x6, waiting for transfers between devices, padded_2(): lax.ppermute(lax.slice_in_dim(block, 0, width, axis=dim), axis, backward)  29.4 us
    unnamed x144, other arithmetic  14.8 us
    ppermute x6, waiting for transfers between devices, padded_2(): lax.ppermute(lax.slice_in_dim(block, block.shape[dim] - width, None, axis...  14.2 us
  transfers between devices with their start and end apart: 12, of which 4 were waited for; matrix products, arithmetic and copies ran while one was open for 1% of the time, Pallas kernels for 0%

commit v1 on v0

v1 whole, which is shorter than its diff:
```python
import functools

import jax
import jax.numpy as jnp
from jax import lax
from jax.experimental import pallas as pl
from jax.experimental.pallas import tpu as pltpu
from jax.sharding import PartitionSpec as P

smoothing = 0.2
MESH = pl.DeviceIdType.MESH
F = 12
L = 48
ROWS = F * L
NZ = 8
LAT = 16
TILES = 9
SLAB = 72
STEPS = 6


def kernel(
    ny, cp_ref, wind_ref, insol_ref, imp_ref, snr_ref, kb_ref, coup_ref, rec_ref,
    out_ref, grad_ref,
    adj, adv, sol, coef, inv, mats, fwd, piv, edge_out, edge_in, swap_out, swap_in,
    send_sem, recv_sem, swap_send, swap_recv,
):
    obj = lax.axis_index("obj")
    tile = lax.axis_index("tile")
    y = tile // NZ
    z = lax.rem(tile, NZ)
    east = lax.rem(y + 1, ny) * NZ + z
    west = lax.rem(y + ny - 1, ny) * NZ + z

    edge_in[...] = jnp.zeros_like(edge_in)
    barrier = pltpu.get_barrier_semaphore()
    for peer in (east, west):
        pl.semaphore_signal(barrier, inc=1, device_id=(obj, peer), device_id_type=MESH)
    for hop in range(1, NZ):
        peer = y * NZ + lax.rem(z + hop, NZ)
        pl.semaphore_signal(barrier, inc=1, device_id=(obj, peer), device_id_type=MESH)

    lane = lax.broadcasted_iota(jnp.int32, (8, 128), 1)
    block = lane // LAT
    inside = lax.rem(lane, LAT)

    for half in range(2):
        rows = pl.ds(half * L, L)
        coef[0, rows] = smoothing + 0.5 * wind_ref[0]
        coef[1, rows] = smoothing - 0.5 * wind_ref[0]
        coef[2, rows] = smoothing + 0.5 * wind_ref[1]
        coef[3, rows] = smoothing - 0.5 * wind_ref[1]

    unit = lax.broadcasted_iota(jnp.int32, (16, 128), 1)
    first = 1.0 / (1.0 + kb_ref[0])
    piv[0] = first
    fwd[0] = (unit == 0).astype(jnp.float32)

    def down(l, before):
        inverse, value = before
        below = kb_ref[l - 1]
        weight = below * inverse
        inverse = 1.0 / (1.0 + below + kb_ref[l] - below * weight)
        value = jnp.where(unit == l, 1.0, 0.0) + weight * value
        piv[l] = inverse
        fwd[l] = value
        return inverse, value

    last = lax.fori_loop(1, L, down, (first, (unit == 0).astype(jnp.float32)))
    bottom = last[1] * last[0]
    inv[pl.ds((L - 1) * 16, 16)] = bottom

    def up(i, after):
        l = L - 2 - i
        value = (fwd[l] + kb_ref[l] * after) * piv[l]
        inv[pl.ds(pl.multiple_of(l * 16, 16), 16)] = value
        return value

    lax.fori_loop(0, L - 1, up, bottom)
    for f in range(F):
        matrix = inv[pl.ds(f, L, stride=16), :]
        high = matrix.astype(jnp.bfloat16)
        mats[f, pl.ds(0, L)] = high
        mats[f, pl.ds(L, L)] = (matrix - high.astype(jnp.float32)).astype(jnp.bfloat16)

    adj[...] = jnp.zeros_like(adj)
    grad_ref[...] = jnp.zeros_like(grad_ref)
    pl.semaphore_wait(barrier, NZ + 1)

    def at(k, j):
        return pl.ds(pl.multiple_of(SLAB * k + 8 * j, 8), 8)

    def share(way, k, j):
        return coef[way, pl.ds(pl.multiple_of((SLAB * k) % L + 8 * j, 8), 8), :]

    def edge_copy(t, way, peer):
        return pltpu.make_async_remote_copy(
            src_ref=edge_out.at[t, way],
            dst_ref=edge_in.at[t, way],
            send_sem=send_sem.at[t, way],
            recv_sem=recv_sem.at[t, way],
            device_id=(obj, peer),
            device_id_type=MESH,
        )

    def step(t, carry):
        s = STEPS - 1 - t
        impulse = jnp.broadcast_to(imp_ref[pl.ds(s, 1), :], (8, 128))

        def pack(j, c):
            held = [jnp.zeros((8, 128), jnp.float32)] * 4
            for k in range(8):
                a = adj[at(k, j), :] + snr_ref[at(k, j), :] * impulse
                adj[at(k, j), :] = a
                shifts = (16 * k, 16 * (k + 1), k, k - 15)
                for way in range(4):
                    moved = share(way, k, j) * a
                    turn = shifts[way] % 128
                    if turn:
                        moved = pltpu.roll(moved, turn, 1)
                    spot = block == k if way < 2 else inside == k
                    held[way] = jnp.where(spot, moved, held[way])
            for way in range(4):
                edge_out[t, way, pl.ds(pl.multiple_of(8 * j, 8), 8), :] = held[way]
            return c

        lax.fori_loop(0, TILES, pack, 0)
        edge_copy(t, 0, west).start()
        edge_copy(t, 1, east).start()

        @pl.when(z > 0)
        def _():
            edge_copy(t, 2, tile - 1).start()

        @pl.when(z < NZ - 1)
        def _():
            edge_copy(t, 3, tile + 1).start()

        def interior(j, c):
            for k in range(8):
                a = adj[at(k, j), :]
                to_west = pltpu.roll(share(0, k, j) * a, 128 - LAT, 1)
                to_east = pltpu.roll(share(1, k, j) * a, LAT, 1)
                to_south = pltpu.roll(share(2, k, j) * a, 127, 1)
                to_north = pltpu.roll(share(3, k, j) * a, 1, 1)
                adv[at(k, j), :] = (
                    (1.0 - 4.0 * smoothing) * a
                    + jnp.where(block < 7, to_west, 0.0)
                    + jnp.where(block > 0, to_east, 0.0)
                    + jnp.where(inside < LAT - 1, to_south, 0.0)
                    + jnp.where(inside > 0, to_north, 0.0)
                )
            return c

        lax.fori_loop(0, TILES, interior, 0)
        edge_copy(t, 0, west).wait()
        edge_copy(t, 1, east).wait()

        @pl.when(z > 0)
        def _():
            edge_copy(t, 2, tile - 1).wait_send()
            edge_copy(t, 3, tile - 1).wait_recv()

        @pl.when(z < NZ - 1)
        def _():
            edge_copy(t, 3, tile + 1).wait_send()
            edge_copy(t, 2, tile + 1).wait_recv()

        def turned(value, amount):
            return pltpu.roll(value, amount % 128, 1) if amount % 128 else value

        def unpack(j, c):
            got = [edge_in[t, way, pl.ds(pl.multiple_of(8 * j, 8), 8), :] for way in range(4)]
            for k in range(8):
                along = jnp.where(
                    block == 7,
                    turned(got[0], 112 - 16 * k),
                    jnp.where(block == 0, turned(got[1], -16 * k), 0.0),
                )
                across = jnp.where(
                    inside == LAT - 1,
                    turned(got[2], 15 - k),
                    jnp.where(inside == 0, turned(got[3], -k), 0.0),
                )
                adv[at(k, j), :] = adv[at(k, j), :] + along + across
            return c

        lax.fori_loop(0, TILES, unpack, 0)

        insol = insol_ref[pl.ds(0, 1), :]
        wide = lax.broadcasted_iota(jnp.int32, (L, 128), 1)
        for f in range(F):
            rows = pl.ds(f * L, L)
            x = adv[rows, :]
            high = x.astype(jnp.bfloat16)
            low = (x - high.astype(jnp.float32)).astype(jnp.bfloat16)
            both = jnp.dot(
                mats[f][:, :L],
                jnp.concatenate([high, low], axis=1),
                preferred_element_type=jnp.float32,
            )
            solved = both[:L, :128] + (both[:L, 128:] + both[L:, :128])
            sol[rows, :] = solved
            total = jnp.sum(solved * insol, axis=1, keepdims=True)
            grad_ref[rows, :] = jnp.where(wide == s, total, grad_ref[rows, :])

        def mix(i, c):
            def spot(g):
                return pl.ds(pl.multiple_of(g * L + 16 * i, 16), 16)

            parts = [sol[spot(f), :] for f in range(F)]
            for g in range(F):
                state = cp_ref[s, g, pl.ds(pl.multiple_of(16 * i, 16), 16), :]
                total = parts[g] - (2.0 * rec_ref[0, g]) * (state.astype(jnp.float32) * parts[g])
                for f in range(F):
                    total = total + coup_ref[f, g] * parts[f]
                adj[spot(g), :] = total
            return c

        lax.fori_loop(0, L // 16, mix, 0)
        return carry

    lax.fori_loop(0, STEPS, step, 0)

    def spread(j, c):
        turned = [
            pltpu.roll(adj[at(k, j), :], 16 * k, 1) if k else adj[at(k, j), :] for k in range(8)
        ]
        for d in range(NZ):
            piece = turned[0]
            for k in range(1, 8):
                piece = jnp.where(block == (d + k) % 8, turned[k], piece)
            swap_out[d, pl.ds(pl.multiple_of(8 * j, 8), 8), :] = piece
        return c

    lax.fori_loop(0, TILES, spread, 0)

    def swap_copy(hop):
        target = lax.rem(z + hop, NZ)
        return pltpu.make_async_remote_copy(
            src_ref=swap_out.at[target],
            dst_ref=swap_in.at[hop],
            send_sem=swap_send.at[hop],
            recv_sem=swap_recv.at[hop],
            device_id=(obj, y * NZ + target),
            device_id_type=MESH,
        )

    for hop in range(1, NZ):
        swap_copy(hop).start()
    swap_in[0] = swap_out[z]
    for hop in range(1, NZ):
        swap_copy(hop).wait()

    def collect(j, c):
        got = [
            pltpu.roll(
                swap_in[hop, pl.ds(pl.multiple_of(8 * j, 8), 8), :],
                lax.rem(128 + 128 - 16 * (z + hop), 128),
                1,
            )
            for hop in range(NZ)
        ]
        for k in range(8):
            held = got[0]
            for hop in range(1, NZ):
                held = jnp.where(block == (k - hop) % 8, got[hop], held)
            out_ref[at(k, j), :] = pltpu.roll(held, lax.rem(16 * z + 128 - 16 * k, 128), 1)
        return c

    lax.fori_loop(0, TILES, collect, 0)


def per_device(
    checkpoints,
    courant,
    insolation,
    region_mask,
    measure_step,
    snr_weight,
    diffusion_number,
    coupling,
    recombination,
):
    tiles = lax.axis_size("tile")
    ny = tiles // NZ
    chunk = checkpoints.shape[2]
    groups = [[row * NZ + z for z in range(NZ)] for row in range(ny)]
    rows = jnp.concatenate(
        [
            checkpoints.reshape(STEPS * F * chunk, 128).astype(jnp.float32),
            courant.reshape(2 * L, 128),
            insolation,
            region_mask[0].astype(jnp.float32),
        ]
    )
    count = rows.shape[0]
    rows = rows.reshape(count, NZ, LAT).transpose(1, 0, 2)
    rows = lax.all_to_all(rows, "tile", 0, 0, axis_index_groups=groups, tiled=True)
    rows = rows.transpose(1, 0, 2).reshape(count, 128)
    own = STEPS * F * chunk
    state = rows[:own].reshape(STEPS, F, chunk, 128).astype(jnp.bfloat16)
    state = lax.all_gather(state, "obj", axis=2, tiled=True)
    wind = rows[own : own + 2 * L].reshape(2, L, 128)
    insol = rows[own + 2 * L :][:1]
    mask = rows[own + 2 * L + 1 :][:1]
    moments = jnp.arange(1, 9, dtype=jnp.int32)
    impulses = (measure_step[0] == moments).astype(jnp.float32)[:, None] * mask
    weights = jnp.broadcast_to(snr_weight.reshape(ROWS, 1), (ROWS, 128))
    rates = jnp.pad(diffusion_number.T, ((0, 1), (0, 4)))
    rates = jnp.broadcast_to(rates[:, :, None], (L, 16, 128))

    vmem = pl.BlockSpec(memory_space=pltpu.VMEM)
    smem = pl.BlockSpec(memory_space=pltpu.SMEM)
    f32 = jnp.float32
    out, sums = pl.pallas_call(
        functools.partial(kernel, ny),
        out_shape=(
            jax.ShapeDtypeStruct((ROWS, 128), f32),
            jax.ShapeDtypeStruct((ROWS, 128), f32),
        ),
        in_specs=[vmem] * 6 + [smem] * 2,
        out_specs=(vmem, vmem),
        scratch_shapes=[
            pltpu.VMEM((ROWS, 128), f32),
            pltpu.VMEM((ROWS, 128), f32),
            pltpu.VMEM((ROWS, 128), f32),
            pltpu.VMEM((4, 2 * L, 128), f32),
            pltpu.VMEM((L * 16, 128), f32),
            pltpu.VMEM((F, 2 * L, 128), jnp.bfloat16),
            pltpu.VMEM((L, 16, 128), f32),
            pltpu.VMEM((L, 16, 128), f32),
            pltpu.VMEM((STEPS, 4, SLAB, 128), f32),
            pltpu.VMEM((STEPS, 4, SLAB, 128), f32),
            pltpu.VMEM((NZ, SLAB, 128), f32),
            pltpu.VMEM((NZ, SLAB, 128), f32),
            pltpu.SemaphoreType.DMA((STEPS, 4)),
            pltpu.SemaphoreType.DMA((STEPS, 4)),
            pltpu.SemaphoreType.DMA((NZ,)),
            pltpu.SemaphoreType.DMA((NZ,)),
        ],
        compiler_params=pltpu.CompilerParams(collective_id=0, has_side_effects=True),
    )(
        state,
        wind,
        jnp.broadcast_to(insol, (8, 128)),
        impulses,
        weights,
        rates,
        coupling,
        recombination[None],
    )
    sums = lax.psum(sums[:, :STEPS].T, "tile") / (tiles * 128)
    return out.reshape(1, F, L, 1, 128), sums.reshape(1, STEPS, F, L)


def solution(mesh):
    return jax.shard_map(
        per_device,
        mesh=mesh,
        in_specs=(
            P(None, None, "obj", "tile", None),
            P(None, None, "tile", None),
            P("tile", None),
            P("obj", "tile", None),
            P("obj"),
            P(),
            P(),
            P(),
            P(),
        ),
        out_specs=(P("obj", None, None, "tile", None), P("obj", None, None, None)),
        check_vma=False,
    )
```

time: 680 us -> 410 us (0.60)
  blocking collectives: 534 us -> 311 us
  Pallas kernels: 0 us -> 56 us
  starting transfers between devices: 55.3 us -> 12.5 us
  waiting for transfers between devices: 43.6 us -> 13 us
  other arithmetic: 26.3 us -> 3.51 us
  matrix products: 9.1 us -> 0 us
    all_gather x6 -> x1, blocking collectives: 305 us -> 73.5 us  [per_device(): state = lax.all_gather(state, 'obj', axis=2, tiled=True)]
    pallas_call x0 -> x1, Pallas kernels: none -> 56 us  [per_device(): pl.pallas_call(functools.partial(kernel, ny), out_shape=(jax.ShapeDtypeSt...]
    ppermute x12 -> x0, starting transfers between devices: 55.3 us -> none  [the longest x6 42.3 us: padded_2(): lax.ppermute(lax.slice_in_dim(block, 0, width, axis=dim), axis, backward)]
    ppermute x12 -> x0, waiting for transfers between devices: 43.6 us -> none  [the longest x6 29.4 us: padded_2(): lax.ppermute(lax.slice_in_dim(block, 0, width, axis=dim), axis, backward)]
    unnamed x144 -> x1, other arithmetic: 14.8 us -> 1.32 us
    all_to_all x0 -> x1, waiting for transfers between devices: none -> 13 us  [per_device(): lax.all_to_all(rows, 'tile', 0, 0, axis_index_groups=groups, tiled=True)]
    all_to_all x0 -> x1, starting transfers between devices: none -> 12.5 us  [per_device(): lax.all_to_all(rows, 'tile', 0, 0, axis_index_groups=groups, tiled=True)]
    psum x1, blocking collectives: 228 us -> 238 us  [per_device(): sums = lax.psum(sums[:, :STEPS].T, 'tile') / (tiles * 128)]
  transfers between devices with their start and end apart: 12 -> 1, of which waited for: 4 -> 1; matrix products, arithmetic and copies ran while one was open for 1% -> 0% of each run, Pallas kernels for 0% -> 0%
where the time goes in v1:
time: 410 us; the launch traced here: 409 us
  blocking collectives  311 us (76%)
  Pallas kernels  56 us (14%)
  waiting for transfers between devices  13 us (3%)
  starting transfers between devices  12.5 us (3%)
  local copies, waits for them, and re-layouts  11.7 us (3%)
    psum x1, blocking collectives, per_device(): sums = lax.psum(sums[:, :STEPS].T, 'tile') / (tiles * 128)  238 us
    all_gather x1, blocking collectives, per_device(): state = lax.all_gather(state, 'obj', axis=2, tiled=True)  73.5 us
    pallas_call x1, Pallas kernels, per_device(): pl.pallas_call(functools.partial(kernel, ny), out_shape=(jax.ShapeDtypeSt...  56 us
    all_to_all x1, waiting for transfers between devices, per_device(): lax.all_to_all(rows, 'tile', 0, 0, axis_index_groups=groups, tiled=True)  13 us
    all_to_all x1, starting transfers between devices, per_device(): lax.all_to_all(rows, 'tile', 0, 0, axis_index_groups=groups, tiled=True)  12.5 us
  transfers between devices with their start and end apart: 1, of which 1 were waited for; matrix products, arithmetic and copies ran while one was open for 0% of the time, Pallas kernels for 0%

profile of v1, /device:TPU:6, one launch (start us, length us, event | category | flops | bytes accessed | tf_op | source)
XLA Modules:
  0.0 409.2 jit_solution(2476600917897768715)
XLA Ops:
  0.6 0.7 convert_reduce_fusion
  1.3 0.2 convert_element_type.42
  1.5 0.5 broadcast.25
  2.0 1.3 reduce.11
  3.3 0.2 concatenate.11
  3.5 0.9 copy.32
  4.5 0.1 concatenate.8
  4.6 1.2 reshape.62
  5.8 0.0 copy-start.1
  5.8 0.0 copy-start.2
  5.8 0.3 copy.33
  6.2 0.8 maximum_bitcast_fusion
  7.0 12.5 %all-to-all-start = ((f32[8,314,16]{1,2,0:T(8,128)}), f32[8,314,16]{1,2,0:T(8,128)S(1)}, u32[]{:S(2)}, u32[]{:S(2)}) async-start(f32[8,314,16]{1,2,0:T(8,128)} %maximum_bitcast_fusion), calls=%async_computation | async-start | bytes 393216 | tf_op jit(solution)/shard_map/all_to_all | solution.py:299
  20.2 0.0 copy-done.1
  20.2 0.1 broadcast_in_dim.26
  20.2 0.0 copy-done.2
  20.2 0.1 copy.43
  20.4 13.0 %all-to-all-done = f32[8,314,16]{1,2,0:T(8,128)S(1)} async-done(((f32[8,314,16]{1,2,0:T(8,128)}), f32[8,314,16]{1,2,0:T(8,128)S(1)}, u32[]{:S(2)}, u32[]{:S(2)}) %all-to-all-start) | async-done | bytes 160800 | tf_op jit(solution)/shard_map/all_to_all | solution.py:299
  33.4 0.1 slice.29
  33.5 0.2 slice_reduce_fusion
  33.7 0.3 copy.36
  34.0 0.4 convert_element_type.39
  34.4 73.5 %all_gather.3 = bf16[6,12,48,128]{3,1,0,2:T(8,128)(2,1)S(1)} all-gather(bf16[6,12,3,128]{3,1,0,2:T(8,128)(2,1)S(1)} %copy.37), channel_id=1, replica_groups=mesh['obj'=16,'tile'=32] {'obj'}, dimensions={2}, use_global_device_ids=true | all-gather | bytes 940032 | tf_op jit(solution)/shard_map/all_gather | solution.py:303
  107.8 1.3 copy.39.cp_ref
  109.1 0.1 reshape.59
  109.2 0.7 copy.40.wind_ref
  109.9 0.1 broadcast_in_dim.24
  110.0 0.1 mul.16
  110.1 0.7 broadcast_multiply_fusion.1.imp_ref
  110.8 0.6 broadcast_in_dim.25.insol_ref
  111.4 0.9 broadcast_in_dim.27.snr_ref
  112.2 0.9 broadcast_in_dim.28.kb_ref
  113.1 56.0 %shard_map.104 = (f32[576,128]{1,0:T(8,128)}, f32[576,128]{1,0:T(8,128)}) custom-call(bf16[6,12,48,128]{3,2,1,0:T(8,128)(2,1)} %copy.39.cp_ref, f32[2,48,128]{2,1,0:T(8,128)} %copy.40.wind_ref, f32[8,128]{1,0:T(8,128)} %broadcast_in_dim.25.insol_ref, f32[8,128]{1,0:T(8,128)} %broadcast_multiply_fusion.1.imp_ref, f32[576,128]{1,0:T(8,128)} %broadcast_in_dim.27.snr_ref, ...), custom_call_target="tpu_custom_call" | custom-call | tf_op jit(solution)/shard_map/pallas_call | solution.py:316
  169.2 0.0 copy-start
  169.2 1.0 slice_bitcast_fusion
  170.2 237.5 %psum.7 = f32[6,576]{0,1:T(8,128)S(1)} all-reduce(f32[6,576]{0,1:T(8,128)S(1)} %slice_bitcast_fusion), channel_id=1, replica_groups=mesh['obj'=16,'tile'=32] {'tile'}, use_global_device_ids=true, to_apply=%region_0.1 | all-reduce | flops 3456 | bytes 27648 | tf_op jit(solution)/shard_map/psum | solution.py:353
  407.8 0.8 copy.42
  408.5 0.0 copy-done
  408.5 0.7 copy.46
  (5 shorter events, 0.1 us)
Async XLA Ops:
  5.8 14.4 %copy-start.1 = (f32[12,48]{1,0:T(8,128)S(1)}, f32[12,48]{1,0:T(8,128)}, u32[]{:S(2)}) copy-start(f32[12,48]{1,0:T(8,128)} %param.14) | copy-start | bytes 6916
  5.8 14.4 %copy-start.2 = (f32[12,47]{1,0:T(8,128)S(1)}, f32[12,47]{1,0:T(8,128)}, u32[]{:S(2)}) copy-start(f32[12,47]{1,0:T(8,128)} %param.15) | copy-start | bytes 6772
  7.0 26.4 %all-to-all-start = ((f32[8,314,16]{1,2,0:T(8,128)}), f32[8,314,16]{1,2,0:T(8,128)S(1)}, u32[]{:S(2)}, u32[]{:S(2)}) async-start(f32[8,314,16]{1,2,0:T(8,128)} %maximum_bitcast_fusion), calls=%async_computation | async-start | bytes 393216 | tf_op jit(solution)/shard_map/all_to_all | solution.py:299
  169.2 239.4 %copy-start = (f32[576,128]{1,0:T(8,128)S(1)}, f32[576,128]{1,0:T(8,128)}, u32[]{:S(2)}) copy-start(f32[576,128]{1,0:T(8,128)} %get-tuple-element.4) | copy-start | bytes 884740

commit v2 on v1

--- a/solution.py
+++ b/solution.py
@@ -23,7 +23,9 @@
     ny, cp_ref, wind_ref, insol_ref, imp_ref, snr_ref, kb_ref, coup_ref, rec_ref,
     out_ref, grad_ref,
     adj, adv, sol, coef, inv, mats, fwd, piv, edge_out, edge_in, swap_out, swap_in,
-    send_sem, recv_sem, swap_send, swap_recv,
+    gathered, loose, state, sum_out, sum_y, part_out, sum_z,
+    send_sem, recv_sem, swap_send, swap_recv, gather_send, gather_recv,
+    y_send, y_recv, z_send, z_recv,
 ):
     obj = lax.axis_index("obj")
     tile = lax.axis_index("tile")
@@ -31,10 +33,23 @@
     z = lax.rem(tile, NZ)
     east = lax.rem(y + 1, ny) * NZ + z
     west = lax.rem(y + ny - 1, ny) * NZ + z
+    x = obj // 4
+    far = lax.rem(obj // 2, 2)
+    core = lax.rem(obj, 2)
+
+    def chunk(at_x, at_far, at_core):
+        return at_x * 4 + at_far * 2 + at_core
+
+    partner = chunk(x, 1 - far, core)
+    other = chunk(x, far, 1 - core)
+    beside = [chunk(lax.rem(x + h, 4), far, core) for h in range(1, 4)]
 
     edge_in[...] = jnp.zeros_like(edge_in)
     barrier = pltpu.get_barrier_semaphore()
-    for peer in (east, west):
+    for peer in [partner, other] + beside:
+        pl.semaphore_signal(barrier, inc=1, device_id=(peer, tile), device_id_type=MESH)
+    for hop in range(1, ny):
+        peer = lax.rem(y + hop, ny) * NZ + z
         pl.semaphore_signal(barrier, inc=1, device_id=(obj, peer), device_id_type=MESH)
     for hop in range(1, NZ):
         peer = y * NZ + lax.rem(z + hop, NZ)
@@ -84,8 +99,82 @@
         mats[f, pl.ds(L, L)] = (matrix - high.astype(jnp.float32)).astype(jnp.bfloat16)
 
     adj[...] = jnp.zeros_like(adj)
-    grad_ref[...] = jnp.zeros_like(grad_ref)
-    pl.semaphore_wait(barrier, NZ + 1)
+    gathered[obj] = cp_ref[...]
+    pl.semaphore_wait(barrier, 5 + ny - 1 + NZ - 1)
+
+    def gather_copy(s, n, slot, peer, source=None):
+        return pltpu.make_async_remote_copy(
+            src_ref=gathered.at[slot, s] if source is None else source,
+            dst_ref=gathered.at[slot, s],
+            send_sem=gather_send.at[s, n],
+            recv_sem=gather_recv.at[s, slot],
+            device_id=(peer, tile),
+            device_id_type=MESH,
+        )
+
+    def near_slots():
+        return [chunk(lax.rem(x + h, 4), w, core) for h in range(1, 4) for w in range(2)]
+
+    def gather_own(s):
+        for n, peer in enumerate([partner] + beside + [other]):
+            gather_copy(s, n, obj, peer, cp_ref.at[s]).start()
+
+    def gather_far(s):
+        gather_copy(s, 0, partner, partner).wait_recv()
+        for n, peer in enumerate(beside + [other]):
+            gather_copy(s, 5 + n, partner, peer).start()
+
+    def gather_near(s):
+        for n, slot in enumerate(near_slots()):
+            gather_copy(s, 9 + n, slot, other).wait_recv()
+            gather_copy(s, 9 + n, slot, other).start()
+
+    def gather_end(s):
+        for at_x in range(4):
+            for w in range(2):
+                gather_copy(s, 0, chunk(at_x, w, 1 - core), other).wait_recv()
+        for slot in range(16):
+            loose[pl.ds(40 * slot, 36), :] = gathered[slot, s].astype(jnp.float32)
+        for f in range(F):
+            for i in range(3):
+                state[pl.ds(f * L + i, 16, stride=3), :] = loose[
+                    pl.ds(3 * f + i, 16, stride=40), :
+                ]
+
+    def send_own(t, c):
+        gather_own(STEPS - 1 - t)
+        return c
+
+    lax.fori_loop(0, STEPS, send_own, 0)
+
+    def y_copy(s, hop):
+        return pltpu.make_async_remote_copy(
+            src_ref=sum_out.at[s],
+            dst_ref=sum_y.at[s, hop - 1],
+            send_sem=y_send.at[s, hop - 1],
+            recv_sem=y_recv.at[s, hop - 1],
+            device_id=(obj, lax.rem(y + hop, ny) * NZ + z),
+            device_id_type=MESH,
+        )
+
+    def z_copy(s, hop):
+        return pltpu.make_async_remote_copy(
+            src_ref=part_out.at[s],
+            dst_ref=sum_z.at[s, hop - 1],
+            send_sem=z_send.at[s, hop - 1],
+            recv_sem=z_recv.at[s, hop - 1],
+            device_id=(obj, y * NZ + lax.rem(z + hop, NZ)),
+            device_id_type=MESH,
+        )
+
+    def sums_on(s):
+        total = sum_out[s]
+        for hop in range(1, ny):
+            y_copy(s, hop).wait()
+            total = total + sum_y[s, hop - 1]
+        part_out[s] = total
+        for hop in range(1, NZ):
+            z_copy(s, hop).start()
 
     def at(k, j):
         return pl.ds(pl.multiple_of(SLAB * k + 8 * j, 8), 8)
@@ -102,6 +191,10 @@
             device_id=(obj, peer),
             device_id_type=MESH,
         )
+
+    gather_far(STEPS - 1)
+    gather_near(STEPS - 1)
+    gather_far(STEPS - 2)
 
     def step(t, carry):
         s = STEPS - 1 - t
@@ -153,6 +246,15 @@
             return c
 
         lax.fori_loop(0, TILES, interior, 0)
+
+        @pl.when(t < STEPS - 1)
+        def _():
+            gather_near(s - 1)
+
+        @pl.when(t < STEPS - 2)
+        def _():
+            gather_far(s - 2)
+
         edge_copy(t, 0, west).wait()
         edge_copy(t, 1, east).wait()
 
@@ -187,8 +289,12 @@
 
         lax.fori_loop(0, TILES, unpack, 0)
 
+        @pl.when(t > 0)
+        def _():
+            sums_on(s + 1)
+
         insol = insol_ref[pl.ds(0, 1), :]
-        wide = lax.broadcasted_iota(jnp.int32, (L, 128), 1)
+        sums = jnp.zeros((8, 128), jnp.float32)
         for f in range(F):
             rows = pl.ds(f * L, L)
             x = adv[rows, :]
@@ -202,7 +308,12 @@
             solved = both[:L, :128] + (both[:L, 128:] + both[L:, :128])
             sol[rows, :] = solved
             total = jnp.sum(solved * insol, axis=1, keepdims=True)
-            grad_ref[rows, :] = jnp.where(wide == s, total, grad_ref[rows, :])
+            for q in range(L // 8):
+                sums = jnp.where(lane == f * (L // 8) + q, total[8 * q : 8 * q + 8], sums)
+        sum_out[s] = sums
+        for hop in range(1, ny):
+            y_copy(s, hop).start()
+        gather_end(s)
 
         def mix(i, c):
             def spot(g):
@@ -210,8 +321,7 @@
 
             parts = [sol[spot(f), :] for f in range(F)]
             for g in range(F):
-                state = cp_ref[s, g, pl.ds(pl.multiple_of(16 * i, 16), 16), :]
-                total = parts[g] - (2.0 * rec_ref[0, g]) * (state.astype(jnp.float32) * parts[g])
+                total = parts[g] - (2.0 * rec_ref[0, g]) * (state[spot(g), :] * parts[g])
                 for f in range(F):
                     total = total + coup_ref[f, g] * parts[f]
                 adj[spot(g), :] = total
@@ -249,6 +359,7 @@
     for hop in range(1, NZ):
         swap_copy(hop).start()
     swap_in[0] = swap_out[z]
+    sums_on(0)
     for hop in range(1, NZ):
         swap_copy(hop).wait()
 
@@ -269,6 +380,18 @@
         return c
 
     lax.fori_loop(0, TILES, collect, 0)
+
+    def finish(s, c):
+        total = part_out[s]
+        for hop in range(1, NZ):
+            z_copy(s, hop).wait()
+            total = total + sum_z[s, hop - 1]
+        grad_ref[s] = total
+        for n in range(15):
+            gather_copy(s, n, obj, other).wait_send()
+        return c
+
+    lax.fori_loop(0, STEPS, finish, 0)
 
 
 def per_device(
@@ -299,8 +422,7 @@
     rows = lax.all_to_all(rows, "tile", 0, 0, axis_index_groups=groups, tiled=True)
     rows = rows.transpose(1, 0, 2).reshape(count, 128)
     own = STEPS * F * chunk
-    state = rows[:own].reshape(STEPS, F, chunk, 128).astype(jnp.bfloat16)
-    state = lax.all_gather(state, "obj", axis=2, tiled=True)
+    state = rows[:own].reshape(STEPS, F * chunk, 128).astype(jnp.bfloat16)
     wind = rows[own : own + 2 * L].reshape(2, L, 128)
     insol = rows[own + 2 * L :][:1]
     mask = rows[own + 2 * L + 1 :][:1]
@@ -317,7 +439,7 @@
         functools.partial(kernel, ny),
         out_shape=(
             jax.ShapeDtypeStruct((ROWS, 128), f32),
-            jax.ShapeDtypeStruct((ROWS, 128), f32),
+            jax.ShapeDtypeStruct((STEPS, 8, 128), f32),
         ),
         in_specs=[vmem] * 6 + [smem] * 2,
         out_specs=(vmem, vmem),
@@ -334,10 +456,23 @@
             pltpu.VMEM((STEPS, 4, SLAB, 128), f32),
             pltpu.VMEM((NZ, SLAB, 128), f32),
             pltpu.VMEM((NZ, SLAB, 128), f32),
+            pltpu.VMEM((16, STEPS, F * chunk, 128), jnp.bfloat16),
+            pltpu.VMEM((16 * 40, 128), f32),
+            pltpu.VMEM((ROWS, 128), f32),
+            pltpu.VMEM((STEPS, 8, 128), f32),
+            pltpu.VMEM((STEPS, ny - 1, 8, 128), f32),
+            pltpu.VMEM((STEPS, 8, 128), f32),
+            pltpu.VMEM((STEPS, NZ - 1, 8, 128), f32),
             pltpu.SemaphoreType.DMA((STEPS, 4)),
             pltpu.SemaphoreType.DMA((STEPS, 4)),
             pltpu.SemaphoreType.DMA((NZ,)),
             pltpu.SemaphoreType.DMA((NZ,)),
+            pltpu.SemaphoreType.DMA((STEPS, 15)),
+            pltpu.SemaphoreType.DMA((STEPS, 16)),
+            pltpu.SemaphoreType.DMA((STEPS, ny - 1)),
+            pltpu.SemaphoreType.DMA((STEPS, ny - 1)),
+            pltpu.SemaphoreType.DMA((STEPS, NZ - 1)),
+            pltpu.SemaphoreType.DMA((STEPS, NZ - 1)),
         ],
         compiler_params=pltpu.CompilerParams(collective_id=0, has_side_effects=True),
     )(
@@ -350,7 +485,7 @@
         coupling,
         recombination[None],
     )
-    sums = lax.psum(sums[:, :STEPS].T, "tile") / (tiles * 128)
+    sums = sums[:, :, : ROWS // 8].transpose(0, 2, 1) / (tiles * 128)
     return out.reshape(1, F, L, 1, 128), sums.reshape(1, STEPS, F, L)
 
 

time: 410 us -> 117 us (0.29)
  blocking collectives: 311 us -> 0 us
  Pallas kernels: 56 us -> 75.4 us
    psum x1 -> x0, blocking collectives: 238 us -> none  [per_device(): sums = lax.psum(sums[:, :STEPS].T, 'tile') / (tiles * 128)]
    all_gather x1 -> x0, blocking collectives: 73.5 us -> none  [per_device(): state = lax.all_gather(state, 'obj', axis=2, tiled=True)]
    pallas_call x1, Pallas kernels: 56 us -> 75.4 us  [per_device(): pl.pallas_call(functools.partial(kernel, ny), out_shape=(jax.ShapeDtypeSt...]
where the time goes in v2:
time: 117 us; the launch traced here: 116 us
  Pallas kernels  75.4 us (64%)
  starting transfers between devices  12.7 us (11%)
  waiting for transfers between devices  12.4 us (11%)
  local copies, waits for them, and re-layouts  10.7 us (9%)
  other arithmetic  2.95 us (3%)
  between operations  1.42 us (1%)
    pallas_call x1, Pallas kernels, per_device(): pl.pallas_call(functools.partial(kernel, ny), out_shape=(jax.ShapeDtypeSt...  75.4 us
    all_to_all x1, starting transfers between devices, per_device(): lax.all_to_all(rows, 'tile', 0, 0, axis_index_groups=groups, tiled=True)  12.7 us
    all_to_all x1, waiting for transfers between devices, per_device(): lax.all_to_all(rows, 'tile', 0, 0, axis_index_groups=groups, tiled=True)  12.4 us
    unnamed x16, local copies, waits for them, and re-layouts  3.08 us
  transfers between devices with their start and end apart: 1, of which 1 were waited for; matrix products, arithmetic and copies ran while one was open for 0% of the time, Pallas kernels for 0%

profile of v2, /device:TPU:6, one launch (start us, length us, event | category | flops | bytes accessed | tf_op | source)
XLA Modules:
  0.0 115.6 jit_solution(8277215040627725793)
XLA Ops:
  0.6 1.2 %reshape.62 = f32[216,8,16]{2,1,0:T(8,128)S(1)} reshape(bf16[6,12,3,1,128]{4,2,3,1,0:T(4,128)(2,1)} %param.9) | data formatting | bytes 165888 | tf_op jit(solution)/shard_map/convert_element_type | solution.py:414
  1.8 0.0 copy-start.1
  1.8 0.3 copy.34
  2.2 0.4 copy-done.1
  2.6 0.1 copy.33
  2.7 0.1 concatenate.8
  2.9 0.0 copy-start.4
  2.9 0.5 broadcast.27
  3.4 0.1 copy-done.4
  3.5 0.7 reduce.11
  4.2 0.0 copy-start.5
  4.2 0.2 concatenate.11
  4.4 0.4 copy-done.5
  4.9 0.2 convert_element_type.41
  5.1 0.8 maximum_bitcast_fusion
  5.9 0.0 copy-start.3
  5.9 12.7 %all-to-all-start = ((f32[8,314,16]{1,2,0:T(8,128)}), f32[8,314,16]{1,2,0:T(8,128)S(1)}, u32[]{:S(2)}, u32[]{:S(2)}) async-start(f32[8,314,16]{1,2,0:T(8,128)} %maximum_bitcast_fusion), calls=%async_computation | async-start | bytes 393216 | tf_op jit(solution)/shard_map/all_to_all | solution.py:422
  19.2 0.0 copy-done.3
  19.2 0.0 copy-start.2
  19.2 0.1 copy.43
  19.3 0.6 copy-done.2
  19.9 0.1 broadcast_in_dim.26
  20.0 12.4 %all-to-all-done = f32[8,314,16]{1,2,0:T(8,128)S(1)} async-done(((f32[8,314,16]{1,2,0:T(8,128)}), f32[8,314,16]{1,2,0:T(8,128)S(1)}, u32[]{:S(2)}, u32[]{:S(2)}) %all-to-all-start) | async-done | bytes 160800 | tf_op jit(solution)/shard_map/all_to_all | solution.py:422
  32.4 0.2 slice_reduce_fusion
  32.7 0.1 slice.29
  32.7 0.1 mul.16
  32.8 0.1 broadcast_in_dim.24
  32.9 0.2 convert_element_type.38
  33.1 0.8 copy.38.cp_ref
  33.9 0.1 reshape.59
  34.1 0.7 copy.39.wind_ref
  34.8 0.7 broadcast_multiply_fusion.imp_ref
  35.4 0.6 broadcast_in_dim.25.insol_ref
  36.0 0.9 broadcast_in_dim.28.kb_ref
  36.9 0.9 broadcast_in_dim.27.snr_ref
  37.8 75.4 %shard_map.104 = (f32[576,128]{1,0:T(8,128)}, f32[6,8,128]{2,1,0:T(8,128)}) custom-call(bf16[6,36,128]{2,1,0:T(8,128)(2,1)} %copy.38.cp_ref, f32[2,48,128]{2,1,0:T(8,128)} %copy.39.wind_ref, f32[8,128]{1,0:T(8,128)} %broadcast_in_dim.25.insol_ref, f32[8,128]{1,0:T(8,128)} %broadcast_multiply_fusion.imp_ref, f32[576,128]{1,0:T(8,128)} %broadcast_in_dim.27.snr_ref, ...), custom_call_target="tpu_custom_call" | custom-call | tf_op jit(solution)/shard_map/pallas_call | solution.py:438
  113.2 0.0 copy-start
  113.2 0.8 multiply_bitcast_fusion
  113.9 0.1 copy.40
  114.1 0.8 reshape.63
  114.8 0.0 copy-done
  114.8 0.7 copy.46
  (4 shorter events, 0.0 us)
Async XLA Ops:
  1.8 0.8 copy-start.1
  2.9 0.7 copy-start.4
  4.2 0.7 copy-start.5
  5.9 13.3 %copy-start.3 = (f32[12,47]{1,0:T(8,128)S(1)}, f32[12,47]{1,0:T(8,128)}, u32[]{:S(2)}) copy-start(f32[12,47]{1,0:T(8,128)} %param.15) | copy-start | bytes 6772
  5.9 26.6 %all-to-all-start = ((f32[8,314,16]{1,2,0:T(8,128)}), f32[8,314,16]{1,2,0:T(8,128)S(1)}, u32[]{:S(2)}, u32[]{:S(2)}) async-start(f32[8,314,16]{1,2,0:T(8,128)} %maximum_bitcast_fusion), calls=%async_computation | async-start | bytes 393216 | tf_op jit(solution)/shard_map/all_to_all | solution.py:422
  19.2 0.7 copy-start.2
  113.2 1.7 %copy-start = (f32[576,128]{1,0:T(8,128)S(1)}, f32[576,128]{1,0:T(8,128)}, u32[]{:S(2)}) copy-start(f32[576,128]{1,0:T(8,128)} %get-tuple-element.4) | copy-start | bytes 884740

commit v3 on v2

--- a/solution.py
+++ b/solution.py
@@ -17,15 +17,17 @@
 TILES = 9
 SLAB = 72
 STEPS = 6
+CHUNK = 36
+PRE = 56
 
 
 def kernel(
-    ny, cp_ref, wind_ref, insol_ref, imp_ref, snr_ref, kb_ref, coup_ref, rec_ref,
+    ny, cp_ref, wind_ref, insol_ref, mask_ref, arrive_ref, snr_ref, kb_ref, coup_ref, rec_ref,
     out_ref, grad_ref,
     adj, adv, sol, coef, inv, mats, fwd, piv, edge_out, edge_in, swap_out, swap_in,
-    gathered, loose, state, sum_out, sum_y, part_out, sum_z,
+    pre, pre_out, pre_in, post, gathered, loose, state, sum_out, sum_y, part_out, sum_z,
     send_sem, recv_sem, swap_send, swap_recv, gather_send, gather_recv,
-    y_send, y_recv, z_send, z_recv,
+    y_send, y_recv, z_send, z_recv, pre_send, pre_recv,
 ):
     obj = lax.axis_index("obj")
     tile = lax.axis_index("tile")
@@ -59,12 +61,66 @@
     block = lane // LAT
     inside = lax.rem(lane, LAT)
 
-    for half in range(2):
-        rows = pl.ds(half * L, L)
-        coef[0, rows] = smoothing + 0.5 * wind_ref[0]
-        coef[1, rows] = smoothing - 0.5 * wind_ref[0]
-        coef[2, rows] = smoothing + 0.5 * wind_ref[1]
-        coef[3, rows] = smoothing - 0.5 * wind_ref[1]
+    def at(k, j, slab=SLAB):
+        return pl.ds(pl.multiple_of(slab * k + 8 * j, 8), 8)
+
+    def spread(source, slab, target):
+        def body(j, c):
+            rolled = [source[at(k, j, slab), :] for k in range(8)]
+            rolled = [pltpu.roll(v, 16 * k, 1) if k else v for k, v in enumerate(rolled)]
+            for d in range(NZ):
+                piece = rolled[0]
+                for k in range(1, 8):
+                    piece = jnp.where(block == (d + k) % 8, rolled[k], piece)
+                target[d, pl.ds(pl.multiple_of(8 * j, 8), 8), :] = piece
+            return c
+
+        lax.fori_loop(0, slab // 8, body, 0)
+
+    def swap_copy(source, target, sent, got, hop):
+        peer = lax.rem(z + hop, NZ)
+        return pltpu.make_async_remote_copy(
+            src_ref=source.at[peer],
+            dst_ref=target.at[hop],
+            send_sem=sent.at[hop],
+            recv_sem=got.at[hop],
+            device_id=(obj, y * NZ + peer),
+            device_id_type=MESH,
+        )
+
+    def collect(source, slab, target):
+        def body(j, c):
+            got = [
+                pltpu.roll(
+                    source[hop, pl.ds(pl.multiple_of(8 * j, 8), 8), :],
+                    lax.rem(256 - 16 * (z + hop), 128),
+                    1,
+                )
+                for hop in range(NZ)
+            ]
+            for k in range(8):
+                held = got[0]
+                for hop in range(1, NZ):
+                    held = jnp.where(block == (k - hop) % 8, got[hop], held)
+                target[at(k, j, slab), :] = pltpu.roll(
+                    held, lax.rem(16 * z + 128 - 16 * k, 128), 1
+                )
+            return c
+
+        lax.fori_loop(0, slab // 8, body, 0)
+
+    pre[...] = jnp.zeros_like(pre)
+    for s in range(STEPS):
+        pre[pl.ds(PRE * s, CHUNK), :] = cp_ref[s].astype(jnp.float32)
+    pre[pl.ds(6 * PRE, L), :] = wind_ref[0]
+    pre[pl.ds(7 * PRE, L), :] = wind_ref[1]
+    pre[pl.ds(6 * PRE + L, 1), :] = insol_ref[...]
+    pre[pl.ds(7 * PRE + L, 1), :] = mask_ref[...].astype(jnp.float32)
+    spread(pre, PRE, pre_out)
+    pl.semaphore_wait(barrier, 5 + ny - 1 + NZ - 1)
+    for hop in range(1, NZ):
+        swap_copy(pre_out, pre_in, pre_send, pre_recv, hop).start()
+    pre_in[0] = pre_out[z]
 
     unit = lax.broadcasted_iota(jnp.int32, (16, 128), 1)
     first = 1.0 / (1.0 + kb_ref[0])
@@ -99,12 +155,15 @@
         mats[f, pl.ds(L, L)] = (matrix - high.astype(jnp.float32)).astype(jnp.bfloat16)
 
     adj[...] = jnp.zeros_like(adj)
-    gathered[obj] = cp_ref[...]
-    pl.semaphore_wait(barrier, 5 + ny - 1 + NZ - 1)
-
-    def gather_copy(s, n, slot, peer, source=None):
+    for hop in range(1, NZ):
+        swap_copy(pre_out, pre_in, pre_send, pre_recv, hop).wait()
+    collect(pre_in, PRE, post)
+    for s in range(STEPS):
+        gathered[obj, s] = post[pl.ds(PRE * s, CHUNK), :].astype(jnp.bfloat16)
+
+    def gather_copy(s, n, slot, peer):
         return pltpu.make_async_remote_copy(
-            src_ref=gathered.at[slot, s] if source is None else source,
+            src_ref=gathered.at[slot, s],
             dst_ref=gathered.at[slot, s],
             send_sem=gather_send.at[s, n],
             recv_sem=gather_recv.at[s, slot],
@@ -117,7 +176,7 @@
 
     def gather_own(s):
         for n, peer in enumerate([partner] + beside + [other]):
-            gather_copy(s, n, obj, peer, cp_ref.at[s]).start()
+            gather_copy(s, n, obj, peer).start()
 
     def gather_far(s):
         gather_copy(s, 0, partner, partner).wait_recv()
@@ -134,7 +193,7 @@
             for w in range(2):
                 gather_copy(s, 0, chunk(at_x, w, 1 - core), other).wait_recv()
         for slot in range(16):
-            loose[pl.ds(40 * slot, 36), :] = gathered[slot, s].astype(jnp.float32)
+            loose[pl.ds(40 * slot, CHUNK), :] = gathered[slot, s].astype(jnp.float32)
         for f in range(F):
             for i in range(3):
                 state[pl.ds(f * L + i, 16, stride=3), :] = loose[
@@ -146,6 +205,14 @@
         return c
 
     lax.fori_loop(0, STEPS, send_own, 0)
+    eastward = post[pl.ds(6 * PRE, L), :]
+    northward = post[pl.ds(7 * PRE, L), :]
+    for half in range(2):
+        rows = pl.ds(half * L, L)
+        coef[0, rows] = smoothing + 0.5 * eastward
+        coef[1, rows] = smoothing - 0.5 * eastward
+        coef[2, rows] = smoothing + 0.5 * northward
+        coef[3, rows] = smoothing - 0.5 * northward
 
     def y_copy(s, hop):
         return pltpu.make_async_remote_copy(
@@ -176,9 +243,6 @@
         for hop in range(1, NZ):
             z_copy(s, hop).start()
 
-    def at(k, j):
-        return pl.ds(pl.multiple_of(SLAB * k + 8 * j, 8), 8)
-
     def share(way, k, j):
         return coef[way, pl.ds(pl.multiple_of((SLAB * k) % L + 8 * j, 8), 8), :]
 
@@ -192,13 +256,12 @@
             device_id_type=MESH,
         )
 
-    gather_far(STEPS - 1)
-    gather_near(STEPS - 1)
-    gather_far(STEPS - 2)
+    insol = post[pl.ds(6 * PRE + L, 1), :]
+    mask = post[pl.ds(7 * PRE + L, 1), :]
 
     def step(t, carry):
         s = STEPS - 1 - t
-        impulse = jnp.broadcast_to(imp_ref[pl.ds(s, 1), :], (8, 128))
+        impulse = jnp.broadcast_to(arrive_ref[pl.ds(s, 1), :] * mask, (8, 128))
 
         def pack(j, c):
             held = [jnp.zeros((8, 128), jnp.float32)] * 4
@@ -247,11 +310,16 @@
 
         lax.fori_loop(0, TILES, interior, 0)
 
-        @pl.when(t < STEPS - 1)
+        @pl.when(t == 0)
+        def _():
+            gather_far(STEPS - 1)
+            gather_far(STEPS - 2)
+
+        @pl.when((t > 0) & (t < STEPS - 1))
         def _():
             gather_near(s - 1)
 
-        @pl.when(t < STEPS - 2)
+        @pl.when((t > 0) & (t < STEPS - 2))
         def _():
             gather_far(s - 2)
 
@@ -293,7 +361,6 @@
         def _():
             sums_on(s + 1)
 
-        insol = insol_ref[pl.ds(0, 1), :]
         sums = jnp.zeros((8, 128), jnp.float32)
         for f in range(F):
             rows = pl.ds(f * L, L)
@@ -313,6 +380,13 @@
         sum_out[s] = sums
         for hop in range(1, ny):
             y_copy(s, hop).start()
+
+        @pl.when(t == 0)
+        def _():
+            gather_near(STEPS - 1)
+            gather_near(STEPS - 2)
+            gather_far(STEPS - 3)
+
         gather_end(s)
 
         def mix(i, c):
@@ -332,54 +406,14 @@
 
     lax.fori_loop(0, STEPS, step, 0)
 
-    def spread(j, c):
-        turned = [
-            pltpu.roll(adj[at(k, j), :], 16 * k, 1) if k else adj[at(k, j), :] for k in range(8)
-        ]
-        for d in range(NZ):
-            piece = turned[0]
-            for k in range(1, 8):
-                piece = jnp.where(block == (d + k) % 8, turned[k], piece)
-            swap_out[d, pl.ds(pl.multiple_of(8 * j, 8), 8), :] = piece
-        return c
-
-    lax.fori_loop(0, TILES, spread, 0)
-
-    def swap_copy(hop):
-        target = lax.rem(z + hop, NZ)
-        return pltpu.make_async_remote_copy(
-            src_ref=swap_out.at[target],
-            dst_ref=swap_in.at[hop],
-            send_sem=swap_send.at[hop],
-            recv_sem=swap_recv.at[hop],
-            device_id=(obj, y * NZ + target),
-            device_id_type=MESH,
-        )
-
+    spread(adj, SLAB, swap_out)
     for hop in range(1, NZ):
-        swap_copy(hop).start()
+        swap_copy(swap_out, swap_in, swap_send, swap_recv, hop).start()
     swap_in[0] = swap_out[z]
     sums_on(0)
     for hop in range(1, NZ):
-        swap_copy(hop).wait()
-
-    def collect(j, c):
-        got = [
-            pltpu.roll(
-                swap_in[hop, pl.ds(pl.multiple_of(8 * j, 8), 8), :],
-                lax.rem(128 + 128 - 16 * (z + hop), 128),
-                1,
-            )
-            for hop in range(NZ)
-        ]
-        for k in range(8):
-            held = got[0]
-            for hop in range(1, NZ):
-                held = jnp.where(block == (k - hop) % 8, got[hop], held)
-            out_ref[at(k, j), :] = pltpu.roll(held, lax.rem(16 * z + 128 - 16 * k, 128), 1)
-        return c
-
-    lax.fori_loop(0, TILES, collect, 0)
+        swap_copy(swap_out, swap_in, swap_send, swap_recv, hop).wait()
+    collect(swap_in, SLAB, out_ref)
 
     def finish(s, c):
         total = part_out[s]
@@ -407,27 +441,9 @@
 ):
     tiles = lax.axis_size("tile")
     ny = tiles // NZ
-    chunk = checkpoints.shape[2]
-    groups = [[row * NZ + z for z in range(NZ)] for row in range(ny)]
-    rows = jnp.concatenate(
-        [
-            checkpoints.reshape(STEPS * F * chunk, 128).astype(jnp.float32),
-            courant.reshape(2 * L, 128),
-            insolation,
-            region_mask[0].astype(jnp.float32),
-        ]
-    )
-    count = rows.shape[0]
-    rows = rows.reshape(count, NZ, LAT).transpose(1, 0, 2)
-    rows = lax.all_to_all(rows, "tile", 0, 0, axis_index_groups=groups, tiled=True)
-    rows = rows.transpose(1, 0, 2).reshape(count, 128)
-    own = STEPS * F * chunk
-    state = rows[:own].reshape(STEPS, F * chunk, 128).astype(jnp.bfloat16)
-    wind = rows[own : own + 2 * L].reshape(2, L, 128)
-    insol = rows[own + 2 * L :][:1]
-    mask = rows[own + 2 * L + 1 :][:1]
     moments = jnp.arange(1, 9, dtype=jnp.int32)
-    impulses = (measure_step[0] == moments).astype(jnp.float32)[:, None] * mask
+    arrive = (measure_step[0] == moments).astype(jnp.float32)
+    arrive = jnp.broadcast_to(arrive[:, None], (8, 128))
     weights = jnp.broadcast_to(snr_weight.reshape(ROWS, 1), (ROWS, 128))
     rates = jnp.pad(diffusion_number.T, ((0, 1), (0, 4)))
     rates = jnp.broadcast_to(rates[:, :, None], (L, 16, 128))
@@ -441,7 +457,7 @@
             jax.ShapeDtypeStruct((ROWS, 128), f32),
             jax.ShapeDtypeStruct((STEPS, 8, 128), f32),
         ),
-        in_specs=[vmem] * 6 + [smem] * 2,
+        in_specs=[vmem] * 7 + [smem] * 2,
         out_specs=(vmem, vmem),
         scratch_shapes=[
             pltpu.VMEM((ROWS, 128), f32),
@@ -456,7 +472,11 @@
             pltpu.VMEM((STEPS, 4, SLAB, 128), f32),
             pltpu.VMEM((NZ, SLAB, 128), f32),
             pltpu.VMEM((NZ, SLAB, 128), f32),
-            pltpu.VMEM((16, STEPS, F * chunk, 128), jnp.bfloat16),
+            pltpu.VMEM((8 * PRE, 128), f32),
+            pltpu.VMEM((NZ, PRE, 128), f32),
+            pltpu.VMEM((NZ, PRE, 128), f32),
+            pltpu.VMEM((8 * PRE, 128), f32),
+            pltpu.VMEM((16, STEPS, CHUNK, 128), jnp.bfloat16),
             pltpu.VMEM((16 * 40, 128), f32),
             pltpu.VMEM((ROWS, 128), f32),
             pltpu.VMEM((STEPS, 8, 128), f32),
@@ -473,13 +493,16 @@
             pltpu.SemaphoreType.DMA((STEPS, ny - 1)),
             pltpu.SemaphoreType.DMA((STEPS, NZ - 1)),
             pltpu.SemaphoreType.DMA((STEPS, NZ - 1)),
+            pltpu.SemaphoreType.DMA((NZ,)),
+            pltpu.SemaphoreType.DMA((NZ,)),
         ],
         compiler_params=pltpu.CompilerParams(collective_id=0, has_side_effects=True),
     )(
-        state,
-        wind,
-        jnp.broadcast_to(insol, (8, 128)),
-        impulses,
+        checkpoints.reshape(STEPS, CHUNK, 128),
+        courant.reshape(2, L, 128),
+        insolation,
+        region_mask[0],
+        arrive,
         weights,
         rates,
         coupling,

time: 117 us -> 105 us (0.90)
  the two profiles are of different devices: /device:TPU:6 before, /device:TPU:1 now
where the time goes in v3:
time: 105 us; the launch traced here: 104 us
  Pallas kernels  96.6 us (92%)
  local copies, waits for them, and re-layouts  5.57 us (5%)
  between operations  1.36 us (1%)
    pallas_call x1, Pallas kernels, per_device(): pl.pallas_call(functools.partial(kernel, ny), out_shape=(jax.ShapeDtypeSt...  96.6 us

profile of v3, /device:TPU:1, one launch (start us, length us, event | category | flops | bytes accessed | tf_op | source)
XLA Modules:
  0.0 104.4 jit_solution(13339619068854921772)
XLA Ops:
  0.6 0.0 copy-start.2
  0.6 0.0 copy-start.1
  1.3 0.7 broadcast_in_dim.10.arrive_ref
  2.0 0.0 copy-done.2
  2.0 0.1 broadcast_in_dim.11
  2.1 0.8 copy.17
  2.9 0.0 copy-done.1
  2.9 0.7 reshape.25.cp_ref
  3.5 0.9 broadcast_in_dim.24.snr_ref
  4.4 0.9 broadcast_in_dim.25.kb_ref
  5.3 96.6 %shard_map.104 = (f32[576,128]{1,0:T(8,128)}, f32[6,8,128]{2,1,0:T(8,128)}) custom-call(bf16[6,36,128]{2,1,0:T(8,128)(2,1)} %reshape.25.cp_ref, f32[2,48,128]{2,1,0:T(8,128)} %bitcast.14, f32[1,128]{1,0:T(1,128)} %insol_ref.1, s32[1,128]{1,0:T(1,128)} %bitcast.16, f32[8,128]{1,0:T(8,128)} %broadcast_in_dim.10.arrive_ref, ...), custom_call_target="tpu_custom_call" | custom-call | tf_op jit(solution)/shard_map/pallas_call | solution.py:454
  102.0 0.0 copy-start
  102.0 0.8 multiply_bitcast_fusion
  102.8 0.1 copy.14
  102.9 0.8 reshape.29
  103.7 0.0 copy-done
  103.7 0.7 copy.20
  (2 shorter events, 0.0 us)
Async XLA Ops:
  0.6 1.4 %copy-start.2 = (f32[12,48]{1,0:T(8,128)S(1)}, f32[12,48]{1,0:T(8,128)}, u32[]{:S(2)}) copy-start(f32[12,48]{1,0:T(8,128)} %param.14) | copy-start | bytes 6916
  0.6 2.2 %copy-start.1 = (bf16[6,12,3,1,128]{4,2,3,1,0:T(4,128)(2,1)S(1)}, bf16[6,12,3,1,128]{4,2,3,1,0:T(4,128)(2,1)}, u32[]{:S(2)}) copy-start(bf16[6,12,3,1,128]{4,2,3,1,0:T(4,128)(2,1)} %param.9) | copy-start | bytes 165892
  102.0 1.7 %copy-start = (f32[576,128]{1,0:T(8,128)S(1)}, f32[576,128]{1,0:T(8,128)}, u32[]{:S(2)}) copy-start(f32[576,128]{1,0:T(8,128)} %get-tuple-element.4) | copy-start | bytes 884740

commit v4 on v3

--- a/solution.py
+++ b/solution.py
@@ -259,6 +259,16 @@
     insol = post[pl.ds(6 * PRE + L, 1), :]
     mask = post[pl.ds(7 * PRE + L, 1), :]
 
+    def sums_of(s):
+        sums = jnp.zeros((8, 128), jnp.float32)
+        for f in range(F):
+            total = jnp.sum(sol[pl.ds(f * L, L), :] * insol, axis=1, keepdims=True)
+            for q in range(L // 8):
+                sums = jnp.where(lane == f * (L // 8) + q, total[8 * q : 8 * q + 8], sums)
+        sum_out[s] = sums
+        for hop in range(1, ny):
+            y_copy(s, hop).start()
+
     def step(t, carry):
         s = STEPS - 1 - t
         impulse = jnp.broadcast_to(arrive_ref[pl.ds(s, 1), :] * mask, (8, 128))
@@ -280,7 +290,7 @@
                 edge_out[t, way, pl.ds(pl.multiple_of(8 * j, 8), 8), :] = held[way]
             return c
 
-        lax.fori_loop(0, TILES, pack, 0)
+        lax.fori_loop(0, TILES, pack, 0, unroll=9)
         edge_copy(t, 0, west).start()
         edge_copy(t, 1, east).start()
 
@@ -308,7 +318,7 @@
                 )
             return c
 
-        lax.fori_loop(0, TILES, interior, 0)
+        lax.fori_loop(0, TILES, interior, 0, unroll=9)
 
         @pl.when(t == 0)
         def _():
@@ -322,6 +332,15 @@
         @pl.when((t > 0) & (t < STEPS - 2))
         def _():
             gather_far(s - 2)
+
+        @pl.when(t > 0)
+        def _():
+            sums_of(s + 1)
+            gather_end(s)
+
+        @pl.when(t > 1)
+        def _():
+            sums_on(s + 2)
 
         edge_copy(t, 0, west).wait()
         edge_copy(t, 1, east).wait()
@@ -355,13 +374,8 @@
                 adv[at(k, j), :] = adv[at(k, j), :] + along + across
             return c
 
-        lax.fori_loop(0, TILES, unpack, 0)
-
-        @pl.when(t > 0)
-        def _():
-            sums_on(s + 1)
-
-        sums = jnp.zeros((8, 128), jnp.float32)
+        lax.fori_loop(0, TILES, unpack, 0, unroll=9)
+
         for f in range(F):
             rows = pl.ds(f * L, L)
             x = adv[rows, :]
@@ -374,20 +388,13 @@
             )
             solved = both[:L, :128] + (both[:L, 128:] + both[L:, :128])
             sol[rows, :] = solved
-            total = jnp.sum(solved * insol, axis=1, keepdims=True)
-            for q in range(L // 8):
-                sums = jnp.where(lane == f * (L // 8) + q, total[8 * q : 8 * q + 8], sums)
-        sum_out[s] = sums
-        for hop in range(1, ny):
-            y_copy(s, hop).start()
 
         @pl.when(t == 0)
         def _():
             gather_near(STEPS - 1)
             gather_near(STEPS - 2)
             gather_far(STEPS - 3)
-
-        gather_end(s)
+            gather_end(STEPS - 1)
 
         def mix(i, c):
             def spot(g):
@@ -401,7 +408,7 @@
                 adj[spot(g), :] = total
             return c
 
-        lax.fori_loop(0, L // 16, mix, 0)
+        lax.fori_loop(0, L // 16, mix, 0, unroll=True)
         return carry
 
     lax.fori_loop(0, STEPS, step, 0)
@@ -409,7 +416,9 @@
     spread(adj, SLAB, swap_out)
     for hop in range(1, NZ):
         swap_copy(swap_out, swap_in, swap_send, swap_recv, hop).start()
+    sums_of(0)
     swap_in[0] = swap_out[z]
+    sums_on(1)
     sums_on(0)
     for hop in range(1, NZ):
         swap_copy(swap_out, swap_in, swap_send, swap_recv, hop).wait()

time: 105 us -> 97.9 us (0.932)
  Pallas kernels: 96.6 us -> 90 us
    pallas_call x1, Pallas kernels: 96.6 us -> 90 us  [per_device(): pl.pallas_call(functools.partial(kernel, ny), out_shape=(jax.ShapeDtypeSt...]
where the time goes in v4:
time: 97.9 us; the launch traced here: 97.7 us
  Pallas kernels  90 us (92%)
  local copies, waits for them, and re-layouts  5.57 us (6%)
  between operations  1.36 us (1%)
    pallas_call x1, Pallas kernels, per_device(): pl.pallas_call(functools.partial(kernel, ny), out_shape=(jax.ShapeDtypeSt...  90 us

profile of v4, /device:TPU:1, one launch (start us, length us, event | category | flops | bytes accessed | tf_op | source)
XLA Modules:
  0.0 97.7 jit_solution(8020973506754428564)
XLA Ops:
  0.6 0.0 copy-start.2
  0.6 0.0 copy-start.1
  1.3 0.7 broadcast_in_dim.10.arrive_ref
  2.0 0.0 copy-done.2
  2.0 0.1 broadcast_in_dim.11
  2.1 0.8 copy.17
  2.9 0.0 copy-done.1
  2.9 0.7 reshape.25.cp_ref
  3.5 0.9 broadcast_in_dim.24.snr_ref
  4.4 0.9 broadcast_in_dim.25.kb_ref
  5.3 90.0 %shard_map.104 = (f32[576,128]{1,0:T(8,128)}, f32[6,8,128]{2,1,0:T(8,128)}) custom-call(bf16[6,36,128]{2,1,0:T(8,128)(2,1)} %reshape.25.cp_ref, f32[2,48,128]{2,1,0:T(8,128)} %bitcast.14, f32[1,128]{1,0:T(1,128)} %insol_ref.1, s32[1,128]{1,0:T(1,128)} %bitcast.16, f32[8,128]{1,0:T(8,128)} %broadcast_in_dim.10.arrive_ref, ...), custom_call_target="tpu_custom_call" | custom-call | tf_op jit(solution)/shard_map/pallas_call | solution.py:463
  95.3 0.0 copy-start
  95.3 0.8 multiply_bitcast_fusion
  96.1 0.1 copy.14
  96.2 0.8 reshape.29
  97.0 0.0 copy-done
  97.0 0.7 copy.20
  (2 shorter events, 0.0 us)
Async XLA Ops:
  0.6 1.4 %copy-start.2 = (f32[12,48]{1,0:T(8,128)S(1)}, f32[12,48]{1,0:T(8,128)}, u32[]{:S(2)}) copy-start(f32[12,48]{1,0:T(8,128)} %param.14) | copy-start | bytes 6916
  0.6 2.2 %copy-start.1 = (bf16[6,12,3,1,128]{4,2,3,1,0:T(4,128)(2,1)S(1)}, bf16[6,12,3,1,128]{4,2,3,1,0:T(4,128)(2,1)}, u32[]{:S(2)}) copy-start(bf16[6,12,3,1,128]{4,2,3,1,0:T(4,128)(2,1)} %param.9) | copy-start | bytes 165892
  95.3 1.7 %copy-start = (f32[576,128]{1,0:T(8,128)S(1)}, f32[576,128]{1,0:T(8,128)}, u32[]{:S(2)}) copy-start(f32[576,128]{1,0:T(8,128)} %get-tuple-element.4) | copy-start | bytes 884740

commit v5 on v4

--- a/solution.py
+++ b/solution.py
@@ -18,7 +18,13 @@
 SLAB = 72
 STEPS = 6
 CHUNK = 36
-PRE = 56
+PRE = 40
+PIECES = (
+    (0, 0, 40, 6, 0), (0, 40, 4, 0, 36), (0, 44, 4, 1, 36),
+    (1, 0, 40, 7, 0), (1, 40, 4, 2, 36), (1, 44, 4, 3, 36),
+)
+INSOL = 4 * PRE + 36
+MASK = 4 * PRE + 37
 
 
 def kernel(
@@ -112,10 +118,10 @@
     pre[...] = jnp.zeros_like(pre)
     for s in range(STEPS):
         pre[pl.ds(PRE * s, CHUNK), :] = cp_ref[s].astype(jnp.float32)
-    pre[pl.ds(6 * PRE, L), :] = wind_ref[0]
-    pre[pl.ds(7 * PRE, L), :] = wind_ref[1]
-    pre[pl.ds(6 * PRE + L, 1), :] = insol_ref[...]
-    pre[pl.ds(7 * PRE + L, 1), :] = mask_ref[...].astype(jnp.float32)
+    for part, level, count, slab, row in PIECES:
+        pre[pl.ds(slab * PRE + row, count), :] = wind_ref[part, pl.ds(level, count), :]
+    pre[pl.ds(INSOL, 1), :] = insol_ref[...]
+    pre[pl.ds(MASK, 1), :] = mask_ref[...].astype(jnp.float32)
     spread(pre, PRE, pre_out)
     pl.semaphore_wait(barrier, 5 + ny - 1 + NZ - 1)
     for hop in range(1, NZ):
@@ -205,14 +211,12 @@
         return c
 
     lax.fori_loop(0, STEPS, send_own, 0)
-    eastward = post[pl.ds(6 * PRE, L), :]
-    northward = post[pl.ds(7 * PRE, L), :]
-    for half in range(2):
-        rows = pl.ds(half * L, L)
-        coef[0, rows] = smoothing + 0.5 * eastward
-        coef[1, rows] = smoothing - 0.5 * eastward
-        coef[2, rows] = smoothing + 0.5 * northward
-        coef[3, rows] = smoothing - 0.5 * northward
+    for part, level, count, slab, row in PIECES:
+        wind = 0.5 * post[pl.ds(slab * PRE + row, count), :]
+        for half in range(2):
+            rows = pl.ds(half * L + level, count)
+            coef[2 * part, rows, :] = smoothing + wind
+            coef[2 * part + 1, rows, :] = smoothing - wind
 
     def y_copy(s, hop):
         return pltpu.make_async_remote_copy(
@@ -256,8 +260,8 @@
             device_id_type=MESH,
         )
 
-    insol = post[pl.ds(6 * PRE + L, 1), :]
-    mask = post[pl.ds(7 * PRE + L, 1), :]
+    insol = post[pl.ds(INSOL, 1), :]
+    mask = post[pl.ds(MASK, 1), :]
 
     def sums_of(s):
         sums = jnp.zeros((8, 128), jnp.float32)

time: 97.9 us -> 91.7 us (0.937)
  the two profiles are of different devices: /device:TPU:1 before, /device:TPU:6 now
where the time goes in v5:
time: 91.7 us; the launch traced here: 89.9 us
  Pallas kernels  82.2 us (90%)
  local copies, waits for them, and re-layouts  5.57 us (6%)
  between operations  1.36 us (1%)
    pallas_call x1, Pallas kernels, per_device(): pl.pallas_call(functools.partial(kernel, ny), out_shape=(jax.ShapeDtypeSt...  82.2 us

profile of v5, /device:TPU:6, one launch (start us, length us, event | category | flops | bytes accessed | tf_op | source)
XLA Modules:
  0.0 89.9 jit_solution(16101864665688110620)
XLA Ops:
  0.6 0.0 copy-start.2
  0.6 0.0 copy-start.1
  1.3 0.7 broadcast_in_dim.10.arrive_ref
  2.0 0.0 copy-done.2
  2.0 0.1 broadcast_in_dim.11
  2.1 0.8 copy.17
  2.9 0.0 copy-done.1
  2.9 0.7 reshape.25.cp_ref
  3.5 0.9 broadcast_in_dim.24.snr_ref
  4.4 0.9 %broadcast_in_dim.25.kb_ref = f32[48,16,128]{2,1,0:T(8,128)} broadcast(f32[48,16]{1,0:T(8,128)S(1)} %pad.4.clone), dimensions={0,1} | broadcast | bytes 396288 | tf_op jit(solution)/shard_map/broadcast_in_dim | solution.py:462
  5.3 82.2 %shard_map.104 = (f32[576,128]{1,0:T(8,128)}, f32[6,8,128]{2,1,0:T(8,128)}) custom-call(bf16[6,36,128]{2,1,0:T(8,128)(2,1)} %reshape.25.cp_ref, f32[2,48,128]{2,1,0:T(8,128)} %bitcast.14, f32[1,128]{1,0:T(1,128)} %insol_ref.1, s32[1,128]{1,0:T(1,128)} %bitcast.16, f32[8,128]{1,0:T(8,128)} %broadcast_in_dim.10.arrive_ref, ...), custom_call_target="tpu_custom_call" | custom-call | tf_op jit(solution)/shard_map/pallas_call | solution.py:467
  87.5 0.0 copy-start
  87.5 0.8 multiply_bitcast_fusion
  88.3 0.1 copy.14
  88.4 0.8 reshape.29
  89.2 0.0 copy-done
  89.2 0.7 copy.20
  (2 shorter events, 0.0 us)
Async XLA Ops:
  0.6 1.4 %copy-start.2 = (f32[12,48]{1,0:T(8,128)S(1)}, f32[12,48]{1,0:T(8,128)}, u32[]{:S(2)}) copy-start(f32[12,48]{1,0:T(8,128)} %param.14) | copy-start | bytes 6916
  0.6 2.2 %copy-start.1 = (bf16[6,12,3,1,128]{4,2,3,1,0:T(4,128)(2,1)S(1)}, bf16[6,12,3,1,128]{4,2,3,1,0:T(4,128)(2,1)}, u32[]{:S(2)}) copy-start(bf16[6,12,3,1,128]{4,2,3,1,0:T(4,128)(2,1)} %param.9) | copy-start | bytes 165892
  87.5 1.7 %copy-start = (f32[576,128]{1,0:T(8,128)S(1)}, f32[576,128]{1,0:T(8,128)}, u32[]{:S(2)}) copy-start(f32[576,128]{1,0:T(8,128)} %get-tuple-element.4) | copy-start | bytes 884740
